TPU v7x, 256 devices: a whole 4x4x8 slice. The times are simulated.
256 devices in a mesh: req: 4 (over y), blk: 16 (over z, x_lo), tp: 4 (over x_hi, core).
Axes of the slice: x: 4 (x_hi: 2, x_lo: 2; x = x_hi * 2 + x_lo), y: 4, z: 8, core: 2. Of those that a mesh axis runs over, the one named last changes fastest.
Arguments:
- tokens: bfloat16 [4, 2048, 5120], P('req', 'blk', 'tp'), may hold values from -6 to 6
- gain: bfloat16 [5120], replicated, may hold values from 0.5 to 1.5
- w_query: bfloat16 [5120, 5120], P('req', 'tp'), may hold values from -0.078125 to 0.078125
- b_query: bfloat16 [5120], P('tp'), may hold values from -4 to 4
- w_keyval: bfloat16 [5120, 2, 1024], P('req', None, 'tp'), may hold values from -0.078125 to 0.078125
- b_keyval: bfloat16 [2, 1024], P(None, 'tp'), may hold values from -3 to 3
- kv_cache: bfloat16 [4, 2, 112, 128, 1024], P('req', None, 'blk', None, 'tp'), may hold values from -400 to 400
- cached_pages: int32 [4], P('req'), may hold values from 1 to 64, as said below
- page_table: int32 [4, 80], P('req'), may hold values from -1 to 111, as said below
Outputs:
- attended: bfloat16 [4, 2048, 5120], P('req', 'blk', 'tp')
- new_cache: bfloat16 [4, 2, 112, 128, 1024], P('req', None, 'blk', None, 'tp')
Inputs may be any that keep to these rules, and one draw needn't show every extreme that they name: `cached_pages`: one request has the most, 64. `page_table`: entry p of a request's row is the slot (owner index of blk times 7 plus slot) of its logical page p for p below its cached pages plus 16, and -1 beyond; the live pages of a request use distinct slots; one index of blk holds at most 4 cached pages of a request; the request with 64 cached pages has exactly 4 on every index of blk.
All inputs are finite; a program needn't handle non-finite values.
Results may differ from a plain program's by a relative error of at most 0.012.
The roundings to bfloat16 on the way count: a program that leaves them out, or rounds other values in their place, can miss the bound.
Values may be sent and summed in bfloat16 or wider, within the bound.
A program may use at most 128 MiB of HBM per device.

v0:
```python
import jax
import jax.numpy as jnp
from jax import lax
from jax.sharding import PartitionSpec as P

HEAD_SIZE = 128
PAGE_TOKENS = 128
epsilon = 1e-06
rope_base = 1000000.0


def normalize(inputs, gain):
    floats = inputs.astype(jnp.float32)
    scaling = lax.rsqrt(jnp.mean(floats * floats, axis=-1, keepdims=True) + epsilon)
    return (floats * scaling * gain.astype(jnp.float32)).astype(jnp.bfloat16)


def apply_rotation(vectors, token_positions):
    halfway = vectors.shape[-1] // 2
    frequency = rope_base ** (-(jnp.arange(halfway, dtype=jnp.float32) * 2.0 / vectors.shape[-1]))
    angles = token_positions[:, None] * frequency[None, :]
    cosine = jnp.cos(angles)[:, None, :]
    sine_part = jnp.sin(angles)[:, None, :]
    leading = vectors[..., :halfway]
    trailing = vectors[..., halfway:]
    return jnp.concatenate(
        [leading * cosine - trailing * sine_part, trailing * cosine + leading * sine_part], axis=-1
    )


def attend(running, query_rows_all, key_rows, value_rows, allowed):
    scaling = HEAD_SIZE ** (-0.5)
    scores = (
        jnp.einsum("rgjd,kgd->rgjk", query_rows_all, key_rows, preferred_element_type=jnp.float32)
        * scaling
    )
    scores = jnp.where(allowed[:, None, None, :], scores, -jnp.inf)
    maxima, totals, blended = running
    fresh_max = jnp.maximum(maxima, jnp.max(scores, axis=-1))
    weights = jnp.exp(scores - fresh_max[..., None])
    decays = jnp.exp(maxima - fresh_max)
    totals = totals * decays + jnp.sum(weights, axis=-1)
    blended = blended * decays[..., None] + jnp.einsum(
        "rgjk,kgd->rgjd",
        weights.astype(jnp.bfloat16),
        value_rows,
        preferred_element_type=jnp.float32,
    )
    return (fresh_max, totals, blended)


def make_fold(usable_all, query_rows_all, kv_heads_local, running, pieces):
    count = pieces.shape[1]
    stride = max((divisor for divisor in (4, 3, 2, 1) if count % divisor == 0))

    def advance(counter, carried):
        segment = lax.dynamic_slice_in_dim(pieces, counter * stride, stride, 1)
        usable = lax.dynamic_slice_in_dim(usable_all, counter * stride, stride)
        key_rows = segment[0].reshape(stride * PAGE_TOKENS, kv_heads_local, HEAD_SIZE)
        value_rows = segment[1].reshape(stride * PAGE_TOKENS, kv_heads_local, HEAD_SIZE)
        allowed = jnp.repeat(usable, PAGE_TOKENS)[None, :]
        return attend(carried, query_rows_all, key_rows, value_rows, allowed)

    return lax.fori_loop(0, count // stride, advance, running)


def body(tokens, gain, w_query, b_query, w_keyval, b_keyval, kv_cache, cached_pages, page_table):
    whole = lax.all_gather(tokens[0], "tp", axis=1, tiled=True)
    normed = normalize(whole, gain)
    rows_here = normed.shape[0]
    query_width = w_query.shape[1]
    kv_width = w_keyval.shape[2]
    pair_width = 2 * kv_width
    pieces = (
        lax.all_gather(w_query, "req", axis=0, tiled=True),
        lax.all_gather(w_keyval, "req", axis=0, tiled=True),
    )
    count = pieces[0].shape[0]
    query_sum = jnp.dot(normed, pieces[0], preferred_element_type=jnp.float32)
    pair_sum = jnp.dot(
        normed, pieces[1].reshape(count, pair_width), preferred_element_type=jnp.float32
    )
    length = cached_pages[0]
    page_map = page_table[0]
    own_index = lax.axis_index("blk")
    cycle_size = lax.axis_size("blk")
    heads_local = query_width // HEAD_SIZE
    kv_heads_local = kv_width // HEAD_SIZE
    queries_per_group = heads_local // kv_heads_local
    token_index = own_index * rows_here + jnp.arange(rows_here, dtype=jnp.int32)
    token_positions = (length * PAGE_TOKENS + token_index).astype(jnp.float32)
    query_full = query_sum + b_query.astype(jnp.float32)
    query_rows_all = apply_rotation(
        query_full.reshape(rows_here, heads_local, HEAD_SIZE), token_positions
    ).astype(jnp.bfloat16)
    query_rows_all = query_rows_all.reshape(rows_here, kv_heads_local, queries_per_group, HEAD_SIZE)
    pair_full = pair_sum + b_keyval.reshape(pair_width).astype(jnp.float32)
    fresh_key = apply_rotation(
        pair_full[:, :kv_width].reshape(rows_here, kv_heads_local, HEAD_SIZE), token_positions
    ).astype(jnp.bfloat16)
    fresh_value = pair_full[:, kv_width:].astype(jnp.bfloat16)
    fresh_pages = jnp.stack([fresh_key.reshape(rows_here, kv_width), fresh_value]).reshape(
        2, rows_here // PAGE_TOKENS, PAGE_TOKENS, kv_width
    )
    every_page = lax.all_gather(fresh_pages, "blk", axis=1, tiled=True)
    new_count = every_page.shape[1]
    fresh_rows = new_count * PAGE_TOKENS
    new_keys = every_page[0].reshape(fresh_rows, kv_heads_local, HEAD_SIZE)
    new_values = every_page[1].reshape(fresh_rows, kv_heads_local, HEAD_SIZE)
    allowed_fresh = jnp.arange(fresh_rows, dtype=jnp.int32)[None, :] <= token_index[:, None]
    starting = (
        jnp.full((rows_here, kv_heads_local, queries_per_group), -jnp.inf, jnp.float32),
        jnp.zeros((rows_here, kv_heads_local, queries_per_group), jnp.float32),
        jnp.zeros((rows_here, kv_heads_local, queries_per_group, HEAD_SIZE), jnp.float32),
    )
    running = attend(starting, query_rows_all, new_keys, new_values, allowed_fresh)
    cache_storage = kv_cache[0]
    slot_count = cache_storage.shape[1]
    new_slots = lax.dynamic_slice_in_dim(page_map, length, new_count)
    chooser = (
        new_slots[None, :]
        == own_index * slot_count + jnp.arange(slot_count, dtype=jnp.int32)[:, None]
    )
    written = jnp.einsum(
        "sj,cjpw->cspw",
        chooser.astype(jnp.bfloat16),
        every_page,
        preferred_element_type=jnp.float32,
    ).astype(jnp.bfloat16)
    landed = jnp.any(chooser, axis=1)
    new_storage = jnp.where(landed[None, :, None, None], written, cache_storage)
    pool_size = cycle_size * slot_count
    live = jnp.arange(page_map.shape[0], dtype=jnp.int32) < length
    matches = (page_map[None, :] == jnp.arange(pool_size, dtype=jnp.int32)[:, None]) & live[None, :]
    valid = jnp.any(matches, axis=1)
    running = make_fold(
        valid,
        query_rows_all,
        kv_heads_local,
        running,
        lax.all_gather(cache_storage, "blk", axis=1, tiled=True),
    )
    maxima, totals, blended = running
    result = (blended / totals[..., None]).reshape(rows_here, query_width).astype(jnp.bfloat16)
    return (result[None], new_storage[None])


def solution(mesh):
    return jax.shard_map(
        body,
        mesh=mesh,
        in_specs=(
            P("req", "blk", "tp"),
            P(),
            P("req", "tp"),
            P("tp"),
            P("req", None, "tp"),
            P(None, "tp"),
            P("req", None, "blk", None, "tp"),
            P("req"),
            P("req", None),
        ),
        out_specs=(P("req", "blk", "tp"), P("req", None, "blk", None, "tp")),
        check_vma=False,
    )
```

profile of v0, /device:TPU:35, one launch (start us, length us, event | category | flops | bytes accessed | tf_op | source)
XLA Modules:
  0.0 774.0 jit_solution(6554469855381495535)
XLA Ops:
  11.2 25.5 %all-gather.13.cloned.1.call-done = bf16[1,128,5120]{2,1,0:T(8,128)(2,1)} async-done(((bf16[1,128,1280]{2,1,0:T(8,128)(2,1)}), bf16[1,128,5120]{2,1,0:T(8,128)(2,1)}) %all-gather.13.cloned.1.call-update) | async-done | bytes 1310736 | tf_op jit(solution)/shard_map/all_gather | solution.py:68
  36.7 1.6 fusion.26
  38.4 59.7 %all-gather.9.cloned.1.call-done = bf16[5120,2,256]{2,1,0:T(2,128)(2,1)} async-done(((bf16[1280,2,256]{2,1,0:T(2,128)(2,1)}), bf16[5120,2,256]{2,1,0:T(2,128)(2,1)}) %all-gather.9.cloned.1.call-update) | async-done | bytes 5242896 | tf_op jit(solution)/shard_map/all_gather | solution.py:76
  98.1 3.5 copy.82
  106.3 60.9 %all-gather.15.cloned.1.call-done = bf16[2,2048,256]{2,1,0:T(8,128)(2,1)} async-done(((bf16[2,128,256]{2,1,0:T(8,128)(2,1)}), bf16[2,2048,256]{2,1,0:T(8,128)(2,1)}) %all-gather.15.cloned.1.call-update) | async-done | bytes 2097168 | tf_op jit(solution)/shard_map/all_gather | solution.py:105
  167.3 1.7 fusion.61
  168.9 1.1 reshape_squeeze.6
  170.7 3.5 fusion.40
  174.2 1.1 copy.66
  175.3 127.5 %all-gather.11.cloned.1.call-done = bf16[5120,1280]{1,0:T(8,128)(2,1)} async-done(((bf16[1280,1280]{1,0:T(8,128)(2,1)}), bf16[5120,1280]{1,0:T(8,128)(2,1)}) %all-gather.11.cloned.1.call-update) | async-done | bytes 13107216 | tf_op jit(solution)/shard_map/all_gather | solution.py:75
  302.8 6.6 convolution_add_fusion
  310.7 1.1 copy.59
  312.1 1.6 fusion.22
  313.7 2.1 fusion.21
  315.9 3.6 fusion.46
  319.4 299.3 %all-gather.17.cloned.1.call-done = bf16[1,2,112,128,256]{4,3,2,1,0:T(8,128)(2,1)} async-done(((bf16[1,2,7,128,256]{4,3,2,1,0:T(8,128)(2,1)}), bf16[1,2,112,128,256]{4,3,2,1,0:T(8,128)(2,1)}) %all-gather.17.cloned.1.call-update) | async-done | bytes 14680080 | tf_op jit(solution)/shard_map/all_gather | solution.py:141
  618.7 146.7 %while.17 = (s32[]{:T(128)}, f32[128,2,5]{0,2,1:T(8,128)S(1)}, f32[128,2,5]{0,2,1:T(8,128)S(1)}, f32[128,2,5,128]{0,3,2,1:T(8,128)}, pred[112]{0:T(512)(128)(4,1...) while((s32[]{:T(128)}, f32[128,2,5]{0,2,1:T(8,128)S(1)}, ...), condition=%wide.region_7.8_spmd, body=%wide.region_4.0_spmd.sunk | while | flops 343083520 | bytes 12208327 | solution.py:64
  618.9 1.1 constant_dynamic-slice_fusion.3
  621.2 2.7 fusion.76
  624.1 1.1 constant_dynamic-slice_fusion.3
  626.5 2.7 fusion.76
  629.3 1.1 constant_dynamic-slice_fusion.3
  631.7 2.7 fusion.76
  634.6 1.1 constant_dynamic-slice_fusion.3
  636.9 2.7 fusion.76
  639.8 1.1 constant_dynamic-slice_fusion.3
  642.2 2.7 fusion.76
  645.1 1.1 constant_dynamic-slice_fusion.3
  647.4 2.7 fusion.76
  650.3 1.1 constant_dynamic-slice_fusion.3
  652.7 2.7 fusion.76
  655.5 1.1 constant_dynamic-slice_fusion.3
  657.9 2.7 fusion.76
  660.8 1.1 constant_dynamic-slice_fusion.3
  663.1 2.7 fusion.76
  668.4 2.7 fusion.76
  671.3 1.1 constant_dynamic-slice_fusion.3
  673.6 2.7 fusion.76
  676.5 1.1 constant_dynamic-slice_fusion.3
  678.9 2.7 fusion.76
  681.7 1.1 constant_dynamic-slice_fusion.3
  684.1 2.7 fusion.76
  689.3 2.7 fusion.76
  692.2 1.1 constant_dynamic-slice_fusion.3
  694.6 2.7 fusion.76
  697.4 1.1 constant_dynamic-slice_fusion.3
  699.8 2.7 fusion.76
  705.0 2.7 fusion.76
  707.9 1.1 constant_dynamic-slice_fusion.3
  710.3 2.7 fusion.76
  713.2 1.1 constant_dynamic-slice_fusion.3
  715.5 2.7 fusion.76
  718.4 1.1 constant_dynamic-slice_fusion.3
  720.8 2.7 fusion.76
  726.0 2.7 fusion.76
  728.9 1.1 constant_dynamic-slice_fusion.3
  731.2 2.7 fusion.76
  736.5 2.7 fusion.76
  741.7 2.7 fusion.76
  746.9 2.7 fusion.76
  752.2 2.7 fusion.76
  757.4 2.7 fusion.76
  762.7 2.7 fusion.76
  765.4 1.1 divide_convert_fusion
  (313 shorter events, 61.1 us)
Async XLA Ops:
  7.2 29.5 %all-gather.13.cloned.1.call-start = ((), (), s32[]{:S(2)}) async-start(), calls=%async_computation.2 | async-start | bytes 1638400 | tf_op jit(solution)/shard_map/all_gather | solution.py:68
  7.9 90.2 %all-gather.9.cloned.1.call-start = ((), (), s32[]{:S(2)}) async-start(), calls=%async_computation | async-start | bytes 6553600 | tf_op jit(solution)/shard_map/all_gather | solution.py:76
  8.6 158.6 %all-gather.15.cloned.1.call-start = ((), (), s32[]{:S(2)}) async-start(), calls=%async_computation.3 | async-start | bytes 2228224 | tf_op jit(solution)/shard_map/all_gather | solution.py:105
  98.1 3.5 copy-start
  102.6 2.4 copy-start.3
  102.6 2.5 copy-start.4
  103.8 199.0 %all-gather.11.cloned.1.call-start = ((), (), s32[]{:S(2)}) async-start(), calls=%async_computation.1 | async-start | bytes 16384000 | tf_op jit(solution)/shard_map/all_gather | solution.py:75
  104.4 514.3 %all-gather.17.cloned.1.call-start = ((), (), s32[]{:S(2)}) async-start(), calls=%async_computation.4 | async-start | bytes 15597568 | tf_op jit(solution)/shard_map/all_gather | solution.py:141
  309.5 2.6 copy-start.2
  309.7 2.4 copy-start.1
Sparse Core Ops, SparseCore 0:
  9.8 26.8 all-gather.12
  38.5 59.5 all-gather.8
  104.0 63.2 all-gather.14
  168.9 133.8 all-gather.10
  304.5 314.2 all-gather.16
where the time goes:
time: 776 us; the launch traced here: 774 us
  waiting for transfers between devices  575 us (74%)
  matrix products  107 us (14%)
  local copies, waits for them, and re-layouts  48.8 us (6%)
  other arithmetic  26.9 us (3%)
  between operations  14.7 us (2%)
    all_gather x1, waiting for transfers between devices, body(): lax.all_gather(cache_storage, 'blk', axis=1, tiled=True)  299 us
    all_gather x1, waiting for transfers between devices, body(): lax.all_gather(w_query, 'req', axis=0, tiled=True)  127 us
    dot_general x29, matrix products, attend(): jnp.einsum('rgjk,kgd->rgjd', weights.astype(jnp.bfloat16), value_rows, pr...  79.7 us
    all_gather x1, waiting for transfers between devices, body(): every_page = lax.all_gather(fresh_pages, 'blk', axis=1, tiled=True)  60.9 us
    all_gather x1, waiting for transfers between devices, body(): lax.all_gather(w_keyval, 'req', axis=0, tiled=True)  59.7 us
    slice x28, local copies, waits for them, and re-layouts, advance(): segment[1].reshape(stride * PAGE_TOKENS, kv_heads_local, HEAD_SIZE)  29.8 us
    all_gather x1, waiting for transfers between devices, body(): whole = lax.all_gather(tokens[0], 'tp', axis=1, tiled=True)  25.5 us
    reduce_sum x29, other arithmetic, attend(): totals = totals * decays + jnp.sum(weights, axis=-1)  18.7 us
  transfers between devices with their start and end apart: 5, of which 5 were waited for; matrix products, arithmetic and copies ran while one was open for 4% of the time, Pallas kernels for 0%

commit v1 on v0

--- a/solution.py
+++ b/solution.py
@@ -72,7 +72,9 @@
     kv_width = w_keyval.shape[2]
     pair_width = 2 * kv_width
     pieces = (
-        lax.all_gather(w_query, "req", axis=0, tiled=True),
+        jnp.concatenate(
+            lax.all_to_all(jnp.stack([w_query] * lax.axis_size("req")), "req", 0, 0), axis=0
+        ),
         lax.all_gather(w_keyval, "req", axis=0, tiled=True),
     )
     count = pieces[0].shape[0]

time: 776 us -> 649 us (0.84)
  waiting for transfers between devices: 575 us -> 436 us
    all_to_all x0 -> x1, waiting for transfers between devices: none -> 142 us  [body(): lax.all_to_all(jnp.stack([w_query] * lax.axis_size('req')), 'req', 0, 0)]
    all_gather x1 -> x0, waiting for transfers between devices: 127 us -> none  [body(): lax.all_gather(w_query, 'req', axis=0, tiled=True)]
    all_gather x1, waiting for transfers between devices: 299 us -> 206 us  [body(): lax.all_gather(cache_storage, 'blk', axis=1, tiled=True)]
    all_gather x1, waiting for transfers between devices: 60.9 us -> 0.02 us  [body(): every_page = lax.all_gather(fresh_pages, 'blk', axis=1, tiled=True)]
  transfers between devices with their start and end apart: 5 -> 5, of which waited for: 5 -> 4; matrix products, arithmetic and copies ran while one was open for 4% -> 5% of each run, Pallas kernels for 0% -> 0%
where the time goes in v1:
time: 649 us; the launch traced here: 646 us
  waiting for transfers between devices  436 us (67%)
  matrix products  107 us (16%)
  local copies, waits for them, and re-layouts  54.3 us (8%)
  other arithmetic  26.2 us (4%)
  between operations  14.7 us (2%)
  starting transfers between devices  6.87 us (1%)
    all_gather x1, waiting for transfers between devices, body(): lax.all_gather(cache_storage, 'blk', axis=1, tiled=True)  206 us
    all_to_all x1, waiting for transfers between devices, body(): lax.all_to_all(jnp.stack([w_query] * lax.axis_size('req')), 'req', 0, 0)  142 us
    dot_general x29, matrix products, attend(): jnp.einsum('rgjk,kgd->rgjd', weights.astype(jnp.bfloat16), value_rows, pr...  80 us
    all_gather x1, waiting for transfers between devices, body(): lax.all_gather(w_keyval, 'req', axis=0, tiled=True)  59.7 us
    slice x28, local copies, waits for them, and re-layouts, advance(): segment[1].reshape(stride * PAGE_TOKENS, kv_heads_local, HEAD_SIZE)  29.8 us
    all_gather x1, waiting for transfers between devices, body(): whole = lax.all_gather(tokens[0], 'tp', axis=1, tiled=True)  25.6 us
    reduce_sum x29, other arithmetic, attend(): totals = totals * decays + jnp.sum(weights, axis=-1)  18.7 us
    dot_general x29, matrix products, attend(): jnp.einsum('rgjd,kgd->rgjk', query_rows_all, key_rows, preferred_element_...  16.1 us
  transfers between devices with their start and end apart: 5, of which 4 were waited for; matrix products, arithmetic and copies ran while one was open for 5% of the time, Pallas kernels for 0%

profile of v1, /device:TPU:35, one launch (start us, length us, event | category | flops | bytes accessed | tf_op | source)
XLA Modules:
  0.0 646.2 jit_solution(9154062852554492085)
XLA Ops:
  11.2 25.6 %all-gather.10.cloned.1.call-done = bf16[1,128,5120]{2,1,0:T(8,128)(2,1)} async-done(((bf16[1,128,1280]{2,1,0:T(8,128)(2,1)}), bf16[1,128,5120]{2,1,0:T(8,128)(2,1)}) %all-gather.10.cloned.1.call-update) | async-done | bytes 1310736 | tf_op jit(solution)/shard_map/all_gather | solution.py:68
  36.7 1.6 fusion.26
  38.4 59.7 %all-gather.8.cloned.1.call-done = bf16[5120,2,256]{2,1,0:T(2,128)(2,1)} async-done(((bf16[1280,2,256]{2,1,0:T(2,128)(2,1)}), bf16[5120,2,256]{2,1,0:T(2,128)(2,1)}) %all-gather.8.cloned.1.call-update) | async-done | bytes 5242896 | tf_op jit(solution)/shard_map/all_gather | solution.py:78
  98.1 3.5 copy.82
  104.4 7.2 %stack.15 = bf16[4,1280,1280]{2,1,0:T(8,128)(2,1)} broadcast(bf16[1280,1280]{1,0:T(8,128)(2,1)} %param.13), dimensions={1,2} | broadcast | bytes 16384000 | tf_op jit(solution)/shard_map/stack | solution.py:76
  111.6 6.7 %all-to-all-start = ((bf16[4,1280,1280]{2,1,0:T(8,128)(2,1)}), bf16[4,1280,1280]{2,1,0:T(8,128)(2,1)}, u32[]{:S(2)}, u32[]{:S(2)}) async-start(bf16[4,1280,1280]{2,1,0:T(8,128)(2,1)} %stack.15), calls=%async_computation | async-start | bytes 26214400 | tf_op jit(solution)/shard_map/all_to_all | solution.py:76
  119.7 142.3 %all-to-all-done = bf16[4,1280,1280]{2,1,0:T(8,128)(2,1)} async-done(((bf16[4,1280,1280]{2,1,0:T(8,128)(2,1)}), bf16[4,1280,1280]{2,1,0:T(8,128)(2,1)}, u32[]{:S(2)}, u32[]{:S(2)}) %all-to-all-start) | async-done | bytes 13107232 | tf_op jit(solution)/shard_map/all_to_all | solution.py:76
  261.9 6.7 %convolution_add_fusion = f32[128,1280]{1,0:T(8,128)S(1)} fusion(bf16[5120,1280]{1,0:T(8,128)(2,1)} %bitcast.10, bf16[1,128,5120]{2,1,0:T(8,128)(2,1)S(1)} %copy-done, f32[5120]{0:T(1024)S(1)} %convert_element_type.74, f32[128]{0:T(128)S(1)} %add_rsqrt_fusion, f32[1280]{0:T(1024)S(1)} %convert_element_type.80), kind=kOutput, calls=%fused_computation.35 | convolution fusion | flops 1680506880 | bytes 15099392 | tf_op jit(solution)/shard_map/dot_general | solution.py:81
  269.6 1.7 fusion.61
  272.3 3.5 fusion.40
  275.8 1.1 copy.66
  277.0 1.6 fusion.22
  278.6 2.1 fusion.21
  280.8 3.6 fusion.46
  284.3 206.1 %all-gather.14.cloned.1.call-done = bf16[1,2,112,128,256]{4,3,2,1,0:T(8,128)(2,1)} async-done(((bf16[1,2,7,128,256]{4,3,2,1,0:T(8,128)(2,1)}), bf16[1,2,112,128,256]{4,3,2,1,0:T(8,128)(2,1)}) %all-gather.14.cloned.1.call-update) | async-done | bytes 14680080 | tf_op jit(solution)/shard_map/all_gather | solution.py:143
  490.5 147.1 %while.17 = (s32[]{:T(128)}, f32[128,2,5]{0,2,1:T(8,128)S(1)}, f32[128,2,5]{0,2,1:T(8,128)S(1)}, f32[128,2,5,128]{0,3,2,1:T(8,128)}, pred[112]{0:T(512)(128)(4,1...) while((s32[]{:T(128)}, f32[128,2,5]{0,2,1:T(8,128)S(1)}, ...), condition=%wide.region_7.8_spmd, body=%wide.region_4.0_spmd.sunk | while | flops 343083520 | bytes 12208335 | solution.py:64
  490.6 1.1 constant_dynamic-slice_fusion.3
  493.0 2.7 fusion.76
  495.9 1.1 constant_dynamic-slice_fusion.3
  498.3 2.7 fusion.76
  501.1 1.1 constant_dynamic-slice_fusion.3
  503.5 2.7 fusion.76
  506.4 1.1 constant_dynamic-slice_fusion.3
  508.8 2.7 fusion.76
  511.7 1.1 constant_dynamic-slice_fusion.3
  514.0 2.7 fusion.76
  516.9 1.1 constant_dynamic-slice_fusion.3
  519.3 2.7 fusion.76
  522.2 1.1 constant_dynamic-slice_fusion.3
  524.5 2.7 fusion.76
  527.4 1.1 constant_dynamic-slice_fusion.3
  529.8 2.7 fusion.76
  532.7 1.1 constant_dynamic-slice_fusion.3
  535.0 2.7 fusion.76
  537.9 1.1 constant_dynamic-slice_fusion.3
  540.3 2.7 fusion.76
  545.6 2.7 fusion.76
  548.4 1.1 constant_dynamic-slice_fusion.3
  550.8 2.7 fusion.76
  553.7 1.1 constant_dynamic-slice_fusion.3
  556.1 2.7 fusion.76
  558.9 1.1 constant_dynamic-slice_fusion.3
  561.3 2.7 fusion.76
  564.2 1.1 constant_dynamic-slice_fusion.3
  566.6 2.7 fusion.76
  569.5 1.1 constant_dynamic-slice_fusion.3
  571.8 2.7 fusion.76
  577.1 2.7 fusion.76
  580.0 1.1 constant_dynamic-slice_fusion.3
  582.3 2.7 fusion.76
  585.2 1.1 constant_dynamic-slice_fusion.3
  587.6 2.7 fusion.76
  590.5 1.1 constant_dynamic-slice_fusion.3
  592.8 2.7 fusion.76
  595.7 1.1 constant_dynamic-slice_fusion.3
  598.1 2.7 fusion.76
  603.4 2.7 fusion.76
  608.6 2.7 fusion.76
  613.9 2.7 fusion.76
  619.1 2.7 fusion.76
  624.4 2.7 fusion.76
  629.6 2.7 fusion.76
  634.9 2.7 fusion.76
  637.6 1.1 divide_convert_fusion
  (311 shorter events, 59.3 us)
Async XLA Ops:
  7.2 29.5 %all-gather.10.cloned.1.call-start = ((), (), s32[]{:S(2)}) async-start(), calls=%async_computation.2 | async-start | bytes 1638400 | tf_op jit(solution)/shard_map/all_gather | solution.py:68
  7.9 90.2 %all-gather.8.cloned.1.call-start = ((), (), s32[]{:S(2)}) async-start(), calls=%async_computation.1 | async-start | bytes 6553600 | tf_op jit(solution)/shard_map/all_gather | solution.py:78
  8.6 261.0 %all-gather.12.cloned.1.call-start = ((), (), s32[]{:S(2)}) async-start(), calls=%async_computation.3 | async-start | bytes 2228224 | tf_op jit(solution)/shard_map/all_gather | solution.py:107
  98.1 3.5 copy-start
  103.8 386.7 %all-gather.14.cloned.1.call-start = ((), (), s32[]{:S(2)}) async-start(), calls=%async_computation.4 | async-start | bytes 15597568 | tf_op jit(solution)/shard_map/all_gather | solution.py:143
  111.6 6.7 %copy-start.2 = (bf16[1280]{0:T(1024)(128)(2,1)S(1)}, bf16[1280]{0:T(1024)(128)(2,1)}, u32[]{:S(2)}) copy-start(bf16[1280]{0:T(1024)(128)(2,1)} %param.14) | copy-start | bytes 7684
  111.6 6.8 %copy-start.3 = (s32[1,80]{1,0:T(1,128)S(1)}, s32[1,80]{1,0:T(1,128)}, u32[]{:S(2)}) copy-start(s32[1,80]{1,0:T(1,128)} %param.19) | copy-start | bytes 964
  111.6 150.3 %all-to-all-start = ((bf16[4,1280,1280]{2,1,0:T(8,128)(2,1)}), bf16[4,1280,1280]{2,1,0:T(8,128)(2,1)}, u32[]{:S(2)}, u32[]{:S(2)}) async-start(bf16[4,1280,1280]{2,1,0:T(8,128)(2,1)} %stack.15), calls=%async_computation | async-start | bytes 26214400 | tf_op jit(solution)/shard_map/all_to_all | solution.py:76
  272.3 4.7 copy-start.1
Sparse Core Ops, SparseCore 0:
  9.8 26.8 all-gather.9
  38.5 59.5 all-gather.7
  103.9 63.2 all-gather.11
  168.9 321.5 all-gather.13
